TPU v7x, 32 devices: a whole 2x2x4 slice. The times are simulated.
32 devices in a mesh: blk: 8 (over y, x, core), rows: 4 (over z).
Axes of the slice: x: 2, y: 2, z: 4, core: 2. Of those that a mesh axis runs over, the one named last changes fastest.
Arguments:
- sens_tiles: bfloat16 [2048, 512, 128], P('blk', 'rows'), may hold values from -1 to 1
- start_basis: bfloat16 [64, 32768], P(None, 'blk'), may hold values from -6 to 6
- row_blocks: int32 [2048, 4], P('blk', 'rows'), may hold values from 0 to 7, as said below
- col_blocks: int32 [2048, 4], P('blk', 'rows'), may hold values from 0 to 31, as said below
- live_counts: int32 [8, 4], P('blk', 'rows'), may hold values from 64 to 256, as said below
Outputs:
- orthonormal: float32 [4, 64, 32768], P(None, None, ('blk', 'rows'))
Inputs may be any that keep to these rules, and one draw needn't show every extreme that they name: Within one device the pairs (row_blocks, col_blocks) of its 256 slots are distinct. Within one device the pairs (row_blocks, col_blocks) of its 256 slots are distinct. Slots 0 to live_counts - 1 of a device hold its tiles; some device has all 256 slots live.
All inputs are finite; a program needn't handle non-finite values.
Results may differ from a plain program's by a relative error of at most 0.012.
The roundings to bfloat16 on the way count: a program that leaves them out, or rounds other values in their place, can miss the bound.
Values may be sent and summed in bfloat16 or wider, within the bound.
A program may use at most 128 MiB of HBM per device.

v0:
```python
import jax
import jax.numpy as jnp
from jax import lax
from jax.sharding import PartitionSpec as P

RB = 8
CB = 32
ITERS = 4


def apply_forward(sens_tiles, basis_now, col_slots, row_onehot):
    vectors = basis_now.shape[0]
    tile_size = sens_tiles.shape[2]
    picked = jnp.take(basis_now.reshape(vectors, CB, tile_size), col_slots, axis=1)
    products = jnp.einsum("kst,sit->ksi", picked, sens_tiles, preferred_element_type=jnp.float32)
    summed = jnp.einsum("ksi,rs->kri", products, row_onehot, precision=lax.Precision.HIGHEST)
    return summed.reshape(vectors, RB * tile_size)


def apply_backward(sens_tiles, image_half, row_slots, col_onehot):
    vectors = image_half.shape[0]
    tile_size = sens_tiles.shape[2]
    picked = jnp.take(image_half.reshape(vectors, RB, tile_size), row_slots, axis=1)
    products = jnp.einsum("ksi,sij->ksj", picked, sens_tiles, preferred_element_type=jnp.float32)
    summed = jnp.einsum("ksj,cs->kcj", products, col_onehot, precision=lax.Precision.HIGHEST)
    return summed.reshape(vectors, CB * tile_size)


def factor_whole(current, total):
    local_gram = jnp.dot(current, current.T, precision=lax.Precision.HIGHEST)
    gram = lax.psum(local_gram, "blk") / total
    lower = jnp.linalg.cholesky(gram)
    return jax.scipy.linalg.solve_triangular(lower, current, lower=True)


def local(sens_tiles, start_basis, row_blocks, col_blocks, live_counts):
    row_slots = row_blocks[:, 0]
    col_slots = col_blocks[:, 0]
    count_live = live_counts[0, 0]
    slot_total = sens_tiles.shape[0]
    tile_size = sens_tiles.shape[2]
    live = jnp.arange(slot_total) < count_live
    row_onehot = ((row_slots[None, :] == jnp.arange(RB)[:, None]) & live[None, :]).astype(
        jnp.float32
    )
    col_onehot = ((col_slots[None, :] == jnp.arange(CB)[:, None]) & live[None, :]).astype(
        jnp.float32
    )
    total = float(CB * tile_size * lax.axis_size("blk"))
    own_width = CB * tile_size // lax.axis_size("rows")
    basis_now = start_basis
    results = []
    for iteration in range(ITERS):
        partial_image = apply_forward(sens_tiles, basis_now, col_slots, row_onehot)
        image = lax.psum(partial_image, "blk")
        image_half = image.astype(jnp.bfloat16)
        partial_hessian = apply_backward(sens_tiles, image_half, row_slots, col_onehot)
        hessian = lax.psum(partial_hessian, "rows")
        whole_result = factor_whole(hessian, total)
        basis_now = whole_result.astype(jnp.bfloat16)
        result = lax.dynamic_slice_in_dim(
            whole_result, lax.axis_index("rows") * own_width, own_width, 1
        )
        results.append(result)
    return jnp.stack(results, axis=0)


def solution(mesh):
    in_specs = (
        P("blk", "rows", None),
        P(None, "blk"),
        P("blk", "rows"),
        P("blk", "rows"),
        P("blk", "rows"),
    )
    out_specs = P(None, None, ("blk", "rows"))
    return jax.shard_map(local, mesh=mesh, in_specs=in_specs, out_specs=out_specs, check_vma=False)
```

profile of v0, /device:TPU:0, one launch (start us, length us, event | category | flops | bytes accessed | tf_op | source)
XLA Modules:
  0.0 653.3 jit_solution(9419659961309902612)
XLA Ops:
  9.5 3.0 gather_fusion
  12.5 10.4 %fusion.48 = f32[64,256,128]{2,0,1:T(8,128)S(1)} fusion(bf16[256,128,128]{2,1,0:T(8,128)(2,1)} %param.12, bf16[256,64,128]{2,1,0:T(8,128)(2,1)} %gather_fusion, pred[256]{0:T(512)(128)(4,1)S(1)} %get-tuple-element.8), kind=kOutput, calls=%fused_computation.56 | convolution fusion | flops 538968064 | bytes 20971776 | tf_op jit(solution)/shard_map/kst,sit->ksi/dot_general | solution.py:15
  22.9 7.5 %fusion.14 = f32[8,64,128]{2,0,1:T(8,128)S(1)} fusion(f32[64,256,128]{2,0,1:T(8,128)S(1)} %fusion.48, s32[256]{0:T(256)S(1)} %bitcast.242, pred[256]{0:T(512)(128)(4,1)S(1)} %iota_compare_fusion.4), kind=kOutput, calls=%fused_computation.22 | convolution fusion | flops 201330688 | bytes 8652032 | tf_op jit(solution)/shard_map/ksi,rs->kri/dot_general | solution.py:16
  30.8 28.4 %all-reduce.16 = bf16[64,1024]{1,0:T(8,128)(2,1)S(1)} all-reduce(f32[64,1024]{1,0:T(8,128)S(1)} %bitcast.236), channel_id=1, replica_groups=mesh['blk'=8,'rows'=4] {'blk'}, use_global_device_ids=true, to_apply=%region_0.0 | all-reduce | flops 65536 | bytes 393216 | tf_op jit(solution)/shard_map/psum | solution.py:55
  59.3 3.0 gather_fusion.1
  62.3 7.0 %fusion.51 = f32[64,256,128]{2,0,1:T(8,128)S(1)} fusion(bf16[256,128,128]{2,1,0:T(8,128)(2,1)} %param.12, bf16[256,64,128]{2,1,0:T(8,128)(2,1)} %gather_fusion.1, pred[256]{0:T(512)(128)(4,1)S(1)} %get-tuple-element.6), kind=kOutput, calls=%fused_computation.57 | convolution fusion | flops 538968064 | bytes 20971776 | tf_op jit(solution)/shard_map/ksi,sij->ksj/dot_general | solution.py:24
  69.4 7.7 %fusion.12 = f32[32,64,128]{2,0,1:T(8,128)S(1)} fusion(f32[64,256,128]{2,0,1:T(8,128)S(1)} %fusion.51, s32[256]{0:T(256)S(1)} %bitcast.248, pred[256]{0:T(512)(128)(4,1)S(1)} %iota_compare_fusion.4), kind=kOutput, calls=%fused_computation.20 | convolution fusion | flops 805322752 | bytes 9438464 | tf_op jit(solution)/shard_map/ksj,cs->kcj/dot_general | solution.py:25
  78.7 51.6 %all-reduce.9.cloned.1.call-done = f32[64,4096]{1,0:T(8,128)} async-done(((f32[64,4096]{1,0:T(8,128)}), f32[64,4096]{1,0:T(8,128)}) %all-reduce.9.cloned.1.call-update) | async-done | bytes 1048592 | tf_op jit(solution)/shard_map/psum | solution.py:58
  130.3 2.5 fusion.116
  132.8 24.3 %psum.86 = f32[64,64]{0,1:T(8,128)S(1)} all-reduce(f32[64,64]{0,1:T(8,128)S(1)} %fusion.116), channel_id=1, replica_groups=mesh['blk'=8,'rows'=4] {'blk'}, use_global_device_ids=true, to_apply=%region_2.0 | all-reduce | flops 4096 | bytes 32768 | tf_op jit(solution)/shard_map/psum | solution.py:31
  157.2 5.8 cholesky.74
  164.4 4.9 custom-call.8
  172.7 3.0 gather_fusion.2
  175.7 10.4 %fusion.54 = f32[64,256,128]{2,0,1:T(8,128)S(1)} fusion(bf16[256,128,128]{2,1,0:T(8,128)(2,1)} %param.12, bf16[256,64,128]{2,1,0:T(8,128)(2,1)} %gather_fusion.2, pred[256]{0:T(512)(128)(4,1)S(1)} %get-tuple-element.8), kind=kOutput, calls=%fused_computation.58 | convolution fusion | flops 538968064 | bytes 20971776 | tf_op jit(solution)/shard_map/kst,sit->ksi/dot_general | solution.py:15
  186.1 7.9 %fusion.10 = f32[8,64,128]{2,0,1:T(8,128)S(1)} fusion(f32[64,256,128]{2,0,1:T(8,128)S(1)} %fusion.54, s32[256]{0:T(256)S(1)} %bitcast.243, pred[256]{0:T(512)(128)(4,1)S(1)} %iota_compare_fusion.4), kind=kOutput, calls=%fused_computation.18 | convolution fusion | flops 201330688 | bytes 8652032 | tf_op jit(solution)/shard_map/ksi,rs->kri/dot_general | solution.py:16
  194.0 25.3 %all-reduce.17 = bf16[64,1024]{1,0:T(8,128)(2,1)S(1)} all-reduce(f32[64,1024]{1,0:T(8,128)S(1)} %bitcast.237), channel_id=1, replica_groups=mesh['blk'=8,'rows'=4] {'blk'}, use_global_device_ids=true, to_apply=%region_5.10 | all-reduce | flops 65536 | bytes 393216 | tf_op jit(solution)/shard_map/psum | solution.py:55
  219.3 3.0 gather_fusion.3
  222.3 7.0 %fusion.57 = f32[64,256,128]{2,0,1:T(8,128)S(1)} fusion(bf16[256,128,128]{2,1,0:T(8,128)(2,1)} %param.12, bf16[256,64,128]{2,1,0:T(8,128)(2,1)} %gather_fusion.3, pred[256]{0:T(512)(128)(4,1)S(1)} %get-tuple-element.6), kind=kOutput, calls=%fused_computation.59 | convolution fusion | flops 538968064 | bytes 20971776 | tf_op jit(solution)/shard_map/ksi,sij->ksj/dot_general | solution.py:24
  229.4 7.7 %fusion.8 = f32[32,64,128]{2,0,1:T(8,128)S(1)} fusion(f32[64,256,128]{2,0,1:T(8,128)S(1)} %fusion.57, s32[256]{0:T(256)S(1)} %bitcast.249, pred[256]{0:T(512)(128)(4,1)S(1)} %iota_compare_fusion.4), kind=kOutput, calls=%fused_computation.16 | convolution fusion | flops 805322752 | bytes 9438464 | tf_op jit(solution)/shard_map/ksj,cs->kcj/dot_general | solution.py:25
  238.8 49.5 %all-reduce.11.cloned.1.call-done = f32[64,4096]{1,0:T(8,128)} async-done(((f32[64,4096]{1,0:T(8,128)}), f32[64,4096]{1,0:T(8,128)}) %all-reduce.11.cloned.1.call-update) | async-done | bytes 1048592 | tf_op jit(solution)/shard_map/psum | solution.py:58
  288.2 2.5 fusion.117
  290.7 24.3 %psum.89 = f32[64,64]{0,1:T(8,128)S(1)} all-reduce(f32[64,64]{0,1:T(8,128)S(1)} %fusion.117), channel_id=1, replica_groups=mesh['blk'=8,'rows'=4] {'blk'}, use_global_device_ids=true, to_apply=%region_7.12 | all-reduce | flops 4096 | bytes 32768 | tf_op jit(solution)/shard_map/psum | solution.py:31
  315.1 5.8 cholesky.85
  322.3 4.9 custom-call.9
  330.6 3.0 gather_fusion.4
  333.6 10.4 %fusion.60 = f32[64,256,128]{2,0,1:T(8,128)S(1)} fusion(bf16[256,128,128]{2,1,0:T(8,128)(2,1)} %param.12, bf16[256,64,128]{2,1,0:T(8,128)(2,1)} %gather_fusion.4, pred[256]{0:T(512)(128)(4,1)S(1)} %get-tuple-element.8), kind=kOutput, calls=%fused_computation.60 | convolution fusion | flops 538968064 | bytes 20971776 | tf_op jit(solution)/shard_map/kst,sit->ksi/dot_general | solution.py:15
  344.0 7.9 %fusion.6 = f32[8,64,128]{2,0,1:T(8,128)S(1)} fusion(f32[64,256,128]{2,0,1:T(8,128)S(1)} %fusion.60, s32[256]{0:T(256)S(1)} %bitcast.244, pred[256]{0:T(512)(128)(4,1)S(1)} %iota_compare_fusion.4), kind=kOutput, calls=%fused_computation.14 | convolution fusion | flops 201330688 | bytes 8652032 | tf_op jit(solution)/shard_map/ksi,rs->kri/dot_general | solution.py:16
  352.0 25.3 %all-reduce.18 = bf16[64,1024]{1,0:T(8,128)(2,1)S(1)} all-reduce(f32[64,1024]{1,0:T(8,128)S(1)} %bitcast.238), channel_id=1, replica_groups=mesh['blk'=8,'rows'=4] {'blk'}, use_global_device_ids=true, to_apply=%region_8.13 | all-reduce | flops 65536 | bytes 393216 | tf_op jit(solution)/shard_map/psum | solution.py:55
  377.3 3.0 gather_fusion.5
  380.3 7.0 %fusion.63 = f32[64,256,128]{2,0,1:T(8,128)S(1)} fusion(bf16[256,128,128]{2,1,0:T(8,128)(2,1)} %param.12, bf16[256,64,128]{2,1,0:T(8,128)(2,1)} %gather_fusion.5, pred[256]{0:T(512)(128)(4,1)S(1)} %get-tuple-element.6), kind=kOutput, calls=%fused_computation.61 | convolution fusion | flops 538968064 | bytes 20971776 | tf_op jit(solution)/shard_map/ksi,sij->ksj/dot_general | solution.py:24
  387.3 7.7 %fusion.4 = f32[32,64,128]{2,0,1:T(8,128)S(1)} fusion(f32[64,256,128]{2,0,1:T(8,128)S(1)} %fusion.63, s32[256]{0:T(256)S(1)} %bitcast.250, pred[256]{0:T(512)(128)(4,1)S(1)} %iota_compare_fusion.4), kind=kOutput, calls=%fused_computation.12 | convolution fusion | flops 805322752 | bytes 9438464 | tf_op jit(solution)/shard_map/ksj,cs->kcj/dot_general | solution.py:25
  396.7 49.5 %all-reduce.13.cloned.1.call-done = f32[64,4096]{1,0:T(8,128)} async-done(((f32[64,4096]{1,0:T(8,128)}), f32[64,4096]{1,0:T(8,128)}) %all-reduce.13.cloned.1.call-update) | async-done | bytes 1048592 | tf_op jit(solution)/shard_map/psum | solution.py:58
  446.2 2.5 fusion.118
  448.7 24.2 %psum.92 = f32[64,64]{0,1:T(8,128)S(1)} all-reduce(f32[64,64]{0,1:T(8,128)S(1)} %fusion.118), channel_id=1, replica_groups=mesh['blk'=8,'rows'=4] {'blk'}, use_global_device_ids=true, to_apply=%region_10.15 | all-reduce | flops 4096 | bytes 32768 | tf_op jit(solution)/shard_map/psum | solution.py:31
  473.1 5.8 cholesky.96
  480.2 4.9 custom-call.10
  488.5 3.0 gather_fusion.6
  491.6 10.4 %fusion.66 = f32[64,256,128]{2,0,1:T(8,128)S(1)} fusion(bf16[256,128,128]{2,1,0:T(8,128)(2,1)} %param.12, bf16[256,64,128]{2,1,0:T(8,128)(2,1)} %gather_fusion.6, pred[256]{0:T(512)(128)(4,1)S(1)} %get-tuple-element.8), kind=kOutput, calls=%fused_computation.62 | convolution fusion | flops 538968064 | bytes 20971776 | tf_op jit(solution)/shard_map/kst,sit->ksi/dot_general | solution.py:15
  501.9 7.7 %fusion.2 = f32[8,64,128]{2,0,1:T(8,128)S(1)} fusion(f32[64,256,128]{2,0,1:T(8,128)S(1)} %fusion.66, s32[256]{0:T(256)S(1)} %bitcast.245, pred[256]{0:T(512)(128)(4,1)S(1)} %iota_compare_fusion.4), kind=kOutput, calls=%fused_computation.10 | convolution fusion | flops 201330688 | bytes 8652032 | tf_op jit(solution)/shard_map/ksi,rs->kri/dot_general | solution.py:16
  509.7 25.3 %all-reduce.19 = bf16[64,1024]{1,0:T(8,128)(2,1)S(1)} all-reduce(f32[64,1024]{1,0:T(8,128)S(1)} %bitcast.239), channel_id=1, replica_groups=mesh['blk'=8,'rows'=4] {'blk'}, use_global_device_ids=true, to_apply=%region_11.16 | all-reduce | flops 65536 | bytes 393216 | tf_op jit(solution)/shard_map/psum | solution.py:55
  535.0 3.0 gather_fusion.7
  538.0 7.0 %fusion.69 = f32[64,256,128]{2,0,1:T(8,128)S(1)} fusion(bf16[256,128,128]{2,1,0:T(8,128)(2,1)} %param.12, bf16[256,64,128]{2,1,0:T(8,128)(2,1)} %gather_fusion.7, pred[256]{0:T(512)(128)(4,1)S(1)} %get-tuple-element.6), kind=kOutput, calls=%fused_computation.63 | convolution fusion | flops 538968064 | bytes 20971776 | tf_op jit(solution)/shard_map/ksi,sij->ksj/dot_general | solution.py:24
  545.1 7.7 %fusion = f32[32,64,128]{2,0,1:T(8,128)S(1)} fusion(f32[64,256,128]{2,0,1:T(8,128)S(1)} %fusion.69, s32[256]{0:T(256)S(1)} %bitcast.251, pred[256]{0:T(512)(128)(4,1)S(1)} %iota_compare_fusion.4), kind=kOutput, calls=%fused_computation.8 | convolution fusion | flops 805322752 | bytes 9438464 | tf_op jit(solution)/shard_map/ksj,cs->kcj/dot_general | solution.py:25
  557.4 46.5 %all-reduce.15.cloned.1.call-done = f32[64,4096]{1,0:T(8,128)} async-done(((f32[64,4096]{1,0:T(8,128)}), f32[64,4096]{1,0:T(8,128)}) %all-reduce.15.cloned.1.call-update) | async-done | bytes 1048592 | tf_op jit(solution)/shard_map/psum | solution.py:58
  603.9 2.8 fusion.119
  606.7 24.1 %psum.95 = f32[64,64]{0,1:T(8,128)S(1)} all-reduce(f32[64,64]{0,1:T(8,128)S(1)} %fusion.119), channel_id=1, replica_groups=mesh['blk'=8,'rows'=4] {'blk'}, use_global_device_ids=true, to_apply=%region_13.18 | all-reduce | flops 4096 | bytes 32768 | tf_op jit(solution)/shard_map/psum | solution.py:31
  630.9 5.8 cholesky.107
  638.1 4.9 custom-call.11
  (77 shorter events, 31.5 us)
Async XLA Ops:
  6.5 2.8 copy-start
  6.5 123.8 %all-reduce.9.cloned.1.call-start = ((), (), s32[]{:S(2)}) async-start(), calls=%async_computation | async-start | bytes 2097152 | tf_op jit(solution)/shard_map/psum | solution.py:58
  12.5 10.4 %copy-start.5 = (s32[256,1]{0,1:T(1,128)S(1)}, s32[256,1]{0,1:T(1,128)}, u32[]{:S(2)}) copy-start(s32[256,1]{0,1:T(1,128)} %param.14) | copy-start | bytes 3076
  62.3 7.0 %copy-start.6 = (s32[256,1]{0,1:T(1,128)S(1)}, s32[256,1]{0,1:T(1,128)}, u32[]{:S(2)}) copy-start(s32[256,1]{0,1:T(1,128)} %param.15) | copy-start | bytes 3076
  78.7 209.5 %all-reduce.11.cloned.1.call-start = ((), (), s32[]{:S(2)}) async-start(), calls=%async_computation.1 | async-start | bytes 2097152 | tf_op jit(solution)/shard_map/psum | solution.py:58
  171.6 1.0 copy-start.2
  238.7 207.5 %all-reduce.13.cloned.1.call-start = ((), (), s32[]{:S(2)}) async-start(), calls=%async_computation.2 | async-start | bytes 2097152 | tf_op jit(solution)/shard_map/psum | solution.py:58
  329.5 1.0 copy-start.3
  396.7 207.2 %all-reduce.15.cloned.1.call-start = ((), (), s32[]{:S(2)}) async-start(), calls=%async_computation.3 | async-start | bytes 2097152 | tf_op jit(solution)/shard_map/psum | solution.py:58
  487.4 1.0 copy-start.4
  554.4 91.9 %copy-start.1 = (bf16[64,4096]{1,0:T(8,128)(2,1)S(1)}, bf16[64,4096]{1,0:T(8,128)(2,1)}, u32[]{:S(2)}) copy-start(bf16[64,4096]{1,0:T(8,128)(2,1)} %param.13) | copy-start | bytes 1572868
Sparse Core Ops, SparseCore 0:
  78.8 51.4 all-reduce.8
  238.8 49.3 all-reduce.10
  396.8 49.3 all-reduce.12
  554.5 49.3 all-reduce.14
where the time goes:
time: 663 us; the launch traced here: 653 us
  blocking collectives  201 us (30%)
  waiting for transfers between devices  197 us (30%)
  matrix products  151 us (23%)
  other arithmetic  51.9 us (8%)
  local copies, waits for them, and re-layouts  37.5 us (6%)
  between operations  14.7 us (2%)
    psum x4, waiting for transfers between devices, local(): hessian = lax.psum(partial_hessian, 'rows')  197 us
    psum x4, blocking collectives, local(): image = lax.psum(partial_image, 'blk')  104 us
    psum x4, blocking collectives, factor_whole(): gram = lax.psum(local_gram, 'blk') / total  96.9 us
    dot_general x4, matrix products, apply_forward(): jnp.einsum('kst,sit->ksi', picked, sens_tiles, preferred_element_type=jnp...  41.5 us
    dot_general x4, matrix products, apply_forward(): jnp.einsum('ksi,rs->kri', products, row_onehot, precision=lax.Precision.H...  31 us
    dot_general x4, matrix products, apply_backward(): jnp.einsum('ksj,cs->kcj', products, col_onehot, precision=lax.Precision.H...  30.9 us
    dot_general x4, matrix products, apply_backward(): jnp.einsum('ksi,sij->ksj', picked, sens_tiles, preferred_element_type=jnp...  28.1 us
    another operation x12, other arithmetic, factor_whole(): lower = jnp.linalg.cholesky(gram)  26.1 us
  transfers between devices with their start and end apart: 4, of which 4 were waited for; matrix products, arithmetic and copies ran while one was open for 0% of the time, Pallas kernels for 0%

commit v1 on v0

--- a/solution.py
+++ b/solution.py
@@ -28,7 +28,7 @@
 
 def factor_whole(current, total):
     local_gram = jnp.dot(current, current.T, precision=lax.Precision.HIGHEST)
-    gram = lax.psum(local_gram, "blk") / total
+    gram = jnp.sum(lax.all_gather(local_gram, "blk"), axis=0) / total
     lower = jnp.linalg.cholesky(gram)
     return jax.scipy.linalg.solve_triangular(lower, current, lower=True)
 

time: 663 us -> 610 us (0.920)
  blocking collectives: 201 us -> 145 us
    psum x4 -> x0, blocking collectives: 96.9 us -> none  [factor_whole(): gram = lax.psum(local_gram, 'blk') / total]
    all_gather x0 -> x4, blocking collectives: none -> 37.6 us  [factor_whole(): gram = jnp.sum(lax.all_gather(local_gram, 'blk'), axis=0) / total]
where the time goes in v1:
time: 610 us; the launch traced here: 601 us
  waiting for transfers between devices  200 us (33%)
  matrix products  151 us (25%)
  blocking collectives  145 us (24%)
  other arithmetic  52 us (9%)
  local copies, waits for them, and re-layouts  37.8 us (6%)
  between operations  14.7 us (2%)
    psum x4, waiting for transfers between devices, local(): hessian = lax.psum(partial_hessian, 'rows')  200 us
    psum x4, blocking collectives, local(): image = lax.psum(partial_image, 'blk')  108 us
    dot_general x4, matrix products, apply_forward(): jnp.einsum('kst,sit->ksi', picked, sens_tiles, preferred_element_type=jnp...  41.5 us
    all_gather x4, blocking collectives, factor_whole(): gram = jnp.sum(lax.all_gather(local_gram, 'blk'), axis=0) / total  37.6 us
    dot_general x4, matrix products, apply_forward(): jnp.einsum('ksi,rs->kri', products, row_onehot, precision=lax.Precision.H...  31 us
    dot_general x4, matrix products, apply_backward(): jnp.einsum('ksj,cs->kcj', products, col_onehot, precision=lax.Precision.H...  30.9 us
    dot_general x4, matrix products, apply_backward(): jnp.einsum('ksi,sij->ksj', picked, sens_tiles, preferred_element_type=jnp...  28.1 us
    another operation x12, other arithmetic, factor_whole(): lower = jnp.linalg.cholesky(gram)  26.1 us
  transfers between devices with their start and end apart: 4, of which 4 were waited for; matrix products, arithmetic and copies ran while one was open for 0% of the time, Pallas kernels for 0%

profile of v1, /device:TPU:0, one launch (start us, length us, event | category | flops | bytes accessed | tf_op | source)
XLA Modules:
  0.0 600.6 jit_solution(15761520218252803862)
XLA Ops:
  9.5 3.0 gather_fusion
  12.5 10.4 %fusion.48 = f32[64,256,128]{2,0,1:T(8,128)S(1)} fusion(bf16[256,128,128]{2,1,0:T(8,128)(2,1)} %param.12, bf16[256,64,128]{2,1,0:T(8,128)(2,1)} %gather_fusion, pred[256]{0:T(512)(128)(4,1)S(1)} %get-tuple-element.8), kind=kOutput, calls=%fused_computation.56 | convolution fusion | flops 538968064 | bytes 20971776 | tf_op jit(solution)/shard_map/kst,sit->ksi/dot_general | solution.py:15
  22.9 7.5 %fusion.14 = f32[8,64,128]{2,0,1:T(8,128)S(1)} fusion(f32[64,256,128]{2,0,1:T(8,128)S(1)} %fusion.48, s32[256]{0:T(256)S(1)} %bitcast.250, pred[256]{0:T(512)(128)(4,1)S(1)} %iota_compare_fusion.4), kind=kOutput, calls=%fused_computation.22 | convolution fusion | flops 201330688 | bytes 8652032 | tf_op jit(solution)/shard_map/ksi,rs->kri/dot_general | solution.py:16
  30.8 28.4 %all-reduce.16 = bf16[64,1024]{1,0:T(8,128)(2,1)S(1)} all-reduce(f32[64,1024]{1,0:T(8,128)S(1)} %bitcast.244), channel_id=1, replica_groups=mesh['blk'=8,'rows'=4] {'blk'}, use_global_device_ids=true, to_apply=%region_0.0 | all-reduce | flops 65536 | bytes 393216 | tf_op jit(solution)/shard_map/psum | solution.py:55
  59.3 3.0 gather_fusion.1
  62.3 7.0 %fusion.51 = f32[64,256,128]{2,0,1:T(8,128)S(1)} fusion(bf16[256,128,128]{2,1,0:T(8,128)(2,1)} %param.12, bf16[256,64,128]{2,1,0:T(8,128)(2,1)} %gather_fusion.1, pred[256]{0:T(512)(128)(4,1)S(1)} %get-tuple-element.6), kind=kOutput, calls=%fused_computation.57 | convolution fusion | flops 538968064 | bytes 20971776 | tf_op jit(solution)/shard_map/ksi,sij->ksj/dot_general | solution.py:24
  69.4 7.7 %fusion.12 = f32[32,64,128]{2,0,1:T(8,128)S(1)} fusion(f32[64,256,128]{2,0,1:T(8,128)S(1)} %fusion.51, s32[256]{0:T(256)S(1)} %bitcast.256, pred[256]{0:T(512)(128)(4,1)S(1)} %iota_compare_fusion.4), kind=kOutput, calls=%fused_computation.20 | convolution fusion | flops 805322752 | bytes 9438464 | tf_op jit(solution)/shard_map/ksj,cs->kcj/dot_general | solution.py:25
  78.7 51.6 %all-reduce.9.cloned.1.call-done = f32[64,4096]{1,0:T(8,128)} async-done(((f32[64,4096]{1,0:T(8,128)}), f32[64,4096]{1,0:T(8,128)}) %all-reduce.9.cloned.1.call-update) | async-done | bytes 1048592 | tf_op jit(solution)/shard_map/psum | solution.py:58
  130.3 2.5 fusion.116
  132.8 9.4 %all-gather = f32[512,64]{1,0:T(8,128)S(1)} all-gather(f32[64,64]{1,0:T(8,128)S(1)} %fusion.116), channel_id=2, replica_groups=mesh['blk'=8,'rows'=4] {'blk'}, dimensions={0}, use_global_device_ids=true | all-gather | bytes 147456 | tf_op jit(solution)/shard_map/all_gather | solution.py:31
  142.5 5.8 cholesky.74
  149.7 4.9 custom-call.8
  157.9 3.0 gather_fusion.2
  161.0 10.4 %fusion.54 = f32[64,256,128]{2,0,1:T(8,128)S(1)} fusion(bf16[256,128,128]{2,1,0:T(8,128)(2,1)} %param.12, bf16[256,64,128]{2,1,0:T(8,128)(2,1)} %gather_fusion.2, pred[256]{0:T(512)(128)(4,1)S(1)} %get-tuple-element.8), kind=kOutput, calls=%fused_computation.58 | convolution fusion | flops 538968064 | bytes 20971776 | tf_op jit(solution)/shard_map/kst,sit->ksi/dot_general | solution.py:15
  171.3 7.9 %fusion.10 = f32[8,64,128]{2,0,1:T(8,128)S(1)} fusion(f32[64,256,128]{2,0,1:T(8,128)S(1)} %fusion.54, s32[256]{0:T(256)S(1)} %bitcast.251, pred[256]{0:T(512)(128)(4,1)S(1)} %iota_compare_fusion.4), kind=kOutput, calls=%fused_computation.18 | convolution fusion | flops 201330688 | bytes 8652032 | tf_op jit(solution)/shard_map/ksi,rs->kri/dot_general | solution.py:16
  179.3 26.4 %all-reduce.17 = bf16[64,1024]{1,0:T(8,128)(2,1)S(1)} all-reduce(f32[64,1024]{1,0:T(8,128)S(1)} %bitcast.245), channel_id=1, replica_groups=mesh['blk'=8,'rows'=4] {'blk'}, use_global_device_ids=true, to_apply=%region_5.10 | all-reduce | flops 65536 | bytes 393216 | tf_op jit(solution)/shard_map/psum | solution.py:55
  205.8 3.0 gather_fusion.3
  208.8 7.0 %fusion.57 = f32[64,256,128]{2,0,1:T(8,128)S(1)} fusion(bf16[256,128,128]{2,1,0:T(8,128)(2,1)} %param.12, bf16[256,64,128]{2,1,0:T(8,128)(2,1)} %gather_fusion.3, pred[256]{0:T(512)(128)(4,1)S(1)} %get-tuple-element.6), kind=kOutput, calls=%fused_computation.59 | convolution fusion | flops 538968064 | bytes 20971776 | tf_op jit(solution)/shard_map/ksi,sij->ksj/dot_general | solution.py:24
  215.8 7.7 %fusion.8 = f32[32,64,128]{2,0,1:T(8,128)S(1)} fusion(f32[64,256,128]{2,0,1:T(8,128)S(1)} %fusion.57, s32[256]{0:T(256)S(1)} %bitcast.257, pred[256]{0:T(512)(128)(4,1)S(1)} %iota_compare_fusion.4), kind=kOutput, calls=%fused_computation.16 | convolution fusion | flops 805322752 | bytes 9438464 | tf_op jit(solution)/shard_map/ksj,cs->kcj/dot_general | solution.py:25
  225.2 50.4 %all-reduce.11.cloned.1.call-done = f32[64,4096]{1,0:T(8,128)} async-done(((f32[64,4096]{1,0:T(8,128)}), f32[64,4096]{1,0:T(8,128)}) %all-reduce.11.cloned.1.call-update) | async-done | bytes 1048592 | tf_op jit(solution)/shard_map/psum | solution.py:58
  275.6 2.5 fusion.117
  278.1 9.4 %all-gather.1 = f32[512,64]{1,0:T(8,128)S(1)} all-gather(f32[64,64]{1,0:T(8,128)S(1)} %fusion.117), channel_id=3, replica_groups=mesh['blk'=8,'rows'=4] {'blk'}, dimensions={0}, use_global_device_ids=true | all-gather | bytes 147456 | tf_op jit(solution)/shard_map/all_gather | solution.py:31
  287.7 5.8 cholesky.85
  294.9 4.9 custom-call.9
  303.2 3.0 gather_fusion.4
  306.3 10.4 %fusion.60 = f32[64,256,128]{2,0,1:T(8,128)S(1)} fusion(bf16[256,128,128]{2,1,0:T(8,128)(2,1)} %param.12, bf16[256,64,128]{2,1,0:T(8,128)(2,1)} %gather_fusion.4, pred[256]{0:T(512)(128)(4,1)S(1)} %get-tuple-element.8), kind=kOutput, calls=%fused_computation.60 | convolution fusion | flops 538968064 | bytes 20971776 | tf_op jit(solution)/shard_map/kst,sit->ksi/dot_general | solution.py:15
  316.6 7.9 %fusion.6 = f32[8,64,128]{2,0,1:T(8,128)S(1)} fusion(f32[64,256,128]{2,0,1:T(8,128)S(1)} %fusion.60, s32[256]{0:T(256)S(1)} %bitcast.252, pred[256]{0:T(512)(128)(4,1)S(1)} %iota_compare_fusion.4), kind=kOutput, calls=%fused_computation.14 | convolution fusion | flops 201330688 | bytes 8652032 | tf_op jit(solution)/shard_map/ksi,rs->kri/dot_general | solution.py:16
  324.6 26.4 %all-reduce.18 = bf16[64,1024]{1,0:T(8,128)(2,1)S(1)} all-reduce(f32[64,1024]{1,0:T(8,128)S(1)} %bitcast.246), channel_id=1, replica_groups=mesh['blk'=8,'rows'=4] {'blk'}, use_global_device_ids=true, to_apply=%region_8.13 | all-reduce | flops 65536 | bytes 393216 | tf_op jit(solution)/shard_map/psum | solution.py:55
  351.0 3.0 gather_fusion.5
  354.1 7.0 %fusion.63 = f32[64,256,128]{2,0,1:T(8,128)S(1)} fusion(bf16[256,128,128]{2,1,0:T(8,128)(2,1)} %param.12, bf16[256,64,128]{2,1,0:T(8,128)(2,1)} %gather_fusion.5, pred[256]{0:T(512)(128)(4,1)S(1)} %get-tuple-element.6), kind=kOutput, calls=%fused_computation.61 | convolution fusion | flops 538968064 | bytes 20971776 | tf_op jit(solution)/shard_map/ksi,sij->ksj/dot_general | solution.py:24
  361.1 7.7 %fusion.4 = f32[32,64,128]{2,0,1:T(8,128)S(1)} fusion(f32[64,256,128]{2,0,1:T(8,128)S(1)} %fusion.63, s32[256]{0:T(256)S(1)} %bitcast.258, pred[256]{0:T(512)(128)(4,1)S(1)} %iota_compare_fusion.4), kind=kOutput, calls=%fused_computation.12 | convolution fusion | flops 805322752 | bytes 9438464 | tf_op jit(solution)/shard_map/ksj,cs->kcj/dot_general | solution.py:25
  370.5 50.3 %all-reduce.13.cloned.1.call-done = f32[64,4096]{1,0:T(8,128)} async-done(((f32[64,4096]{1,0:T(8,128)}), f32[64,4096]{1,0:T(8,128)}) %all-reduce.13.cloned.1.call-update) | async-done | bytes 1048592 | tf_op jit(solution)/shard_map/psum | solution.py:58
  420.8 2.5 fusion.118
  423.4 9.4 %all-gather.2 = f32[512,64]{1,0:T(8,128)S(1)} all-gather(f32[64,64]{1,0:T(8,128)S(1)} %fusion.118), channel_id=4, replica_groups=mesh['blk'=8,'rows'=4] {'blk'}, dimensions={0}, use_global_device_ids=true | all-gather | bytes 147456 | tf_op jit(solution)/shard_map/all_gather | solution.py:31
  433.0 5.8 cholesky.96
  440.2 4.9 custom-call.10
  448.5 3.0 gather_fusion.6
  451.5 10.4 %fusion.66 = f32[64,256,128]{2,0,1:T(8,128)S(1)} fusion(bf16[256,128,128]{2,1,0:T(8,128)(2,1)} %param.12, bf16[256,64,128]{2,1,0:T(8,128)(2,1)} %gather_fusion.6, pred[256]{0:T(512)(128)(4,1)S(1)} %get-tuple-element.8), kind=kOutput, calls=%fused_computation.62 | convolution fusion | flops 538968064 | bytes 20971776 | tf_op jit(solution)/shard_map/kst,sit->ksi/dot_general | solution.py:15
  461.9 7.7 %fusion.2 = f32[8,64,128]{2,0,1:T(8,128)S(1)} fusion(f32[64,256,128]{2,0,1:T(8,128)S(1)} %fusion.66, s32[256]{0:T(256)S(1)} %bitcast.253, pred[256]{0:T(512)(128)(4,1)S(1)} %iota_compare_fusion.4), kind=kOutput, calls=%fused_computation.10 | convolution fusion | flops 201330688 | bytes 8652032 | tf_op jit(solution)/shard_map/ksi,rs->kri/dot_general | solution.py:16
  469.7 26.4 %all-reduce.19 = bf16[64,1024]{1,0:T(8,128)(2,1)S(1)} all-reduce(f32[64,1024]{1,0:T(8,128)S(1)} %bitcast.247), channel_id=1, replica_groups=mesh['blk'=8,'rows'=4] {'blk'}, use_global_device_ids=true, to_apply=%region_11.16 | all-reduce | flops 65536 | bytes 393216 | tf_op jit(solution)/shard_map/psum | solution.py:55
  496.1 3.0 gather_fusion.7
  499.1 7.0 %fusion.69 = f32[64,256,128]{2,0,1:T(8,128)S(1)} fusion(bf16[256,128,128]{2,1,0:T(8,128)(2,1)} %param.12, bf16[256,64,128]{2,1,0:T(8,128)(2,1)} %gather_fusion.7, pred[256]{0:T(512)(128)(4,1)S(1)} %get-tuple-element.6), kind=kOutput, calls=%fused_computation.63 | convolution fusion | flops 538968064 | bytes 20971776 | tf_op jit(solution)/shard_map/ksi,sij->ksj/dot_general | solution.py:24
  506.2 7.7 %fusion = f32[32,64,128]{2,0,1:T(8,128)S(1)} fusion(f32[64,256,128]{2,0,1:T(8,128)S(1)} %fusion.69, s32[256]{0:T(256)S(1)} %bitcast.259, pred[256]{0:T(512)(128)(4,1)S(1)} %iota_compare_fusion.4), kind=kOutput, calls=%fused_computation.8 | convolution fusion | flops 805322752 | bytes 9438464 | tf_op jit(solution)/shard_map/ksj,cs->kcj/dot_general | solution.py:25
  518.5 47.4 %all-reduce.15.cloned.1.call-done = f32[64,4096]{1,0:T(8,128)} async-done(((f32[64,4096]{1,0:T(8,128)}), f32[64,4096]{1,0:T(8,128)}) %all-reduce.15.cloned.1.call-update) | async-done | bytes 1048592 | tf_op jit(solution)/shard_map/psum | solution.py:58
  565.9 2.8 fusion.119
  568.7 9.3 %all-gather.3 = f32[512,64]{1,0:T(8,128)S(1)} all-gather(f32[64,64]{1,0:T(8,128)S(1)} %fusion.119), channel_id=5, replica_groups=mesh['blk'=8,'rows'=4] {'blk'}, dimensions={0}, use_global_device_ids=true | all-gather | bytes 147456 | tf_op jit(solution)/shard_map/all_gather | solution.py:31
  578.2 5.8 cholesky.107
  585.4 4.9 custom-call.11
  (85 shorter events, 32.0 us)
Async XLA Ops:
  6.5 2.8 copy-start
  6.5 123.8 %all-reduce.9.cloned.1.call-start = ((), (), s32[]{:S(2)}) async-start(), calls=%async_computation | async-start | bytes 2097152 | tf_op jit(solution)/shard_map/psum | solution.py:58
  12.5 10.4 %copy-start.5 = (s32[256,1]{0,1:T(1,128)S(1)}, s32[256,1]{0,1:T(1,128)}, u32[]{:S(2)}) copy-start(s32[256,1]{0,1:T(1,128)} %param.14) | copy-start | bytes 3076
  62.3 7.0 %copy-start.6 = (s32[256,1]{0,1:T(1,128)S(1)}, s32[256,1]{0,1:T(1,128)}, u32[]{:S(2)}) copy-start(s32[256,1]{0,1:T(1,128)} %param.15) | copy-start | bytes 3076
  78.7 196.9 %all-reduce.11.cloned.1.call-start = ((), (), s32[]{:S(2)}) async-start(), calls=%async_computation.1 | async-start | bytes 2097152 | tf_op jit(solution)/shard_map/psum | solution.py:58
  156.8 1.0 copy-start.2
  225.1 195.7 %all-reduce.13.cloned.1.call-start = ((), (), s32[]{:S(2)}) async-start(), calls=%async_computation.2 | async-start | bytes 2097152 | tf_op jit(solution)/shard_map/psum | solution.py:58
  302.1 1.0 copy-start.3
  370.4 195.5 %all-reduce.15.cloned.1.call-start = ((), (), s32[]{:S(2)}) async-start(), calls=%async_computation.3 | async-start | bytes 2097152 | tf_op jit(solution)/shard_map/psum | solution.py:58
  447.4 1.0 copy-start.4
  516.5 77.1 %copy-start.1 = (bf16[64,4096]{1,0:T(8,128)(2,1)S(1)}, bf16[64,4096]{1,0:T(8,128)(2,1)}, u32[]{:S(2)}) copy-start(bf16[64,4096]{1,0:T(8,128)(2,1)} %param.13) | copy-start | bytes 1572868
Sparse Core Ops, SparseCore 0:
  78.8 51.4 all-reduce.8
  225.3 50.2 all-reduce.10
  370.6 50.2 all-reduce.12
  515.6 50.2 all-reduce.14
